TPU v7x, 32 devices: a whole 2x2x4 slice. The times are simulated.
32 devices in a mesh: expert: 16 (over z, y, x), dp: 2 (over core).
Axes of the slice: x: 2, y: 2, z: 4, core: 2. Of those that a mesh axis runs over, the one named last changes fastest.
Arguments:
- tokens: bfloat16 [2048, 2048], P(('expert', 'dp')), may hold values from -6 to 6
- expert_ids: int32 [2048, 8], P(('expert', 'dp')), may hold values from 0 to 15, all different within a row; in each aligned block of 64 rows (0 to 63, 64 to 127, ...) at most 48 rows name the same one
- gate_probs: float32 [2048, 8], P(('expert', 'dp')), may hold values from 0.05 to 1
- swap_flags: int32 [8], replicated, may hold values from 0 to 1, as said below
- w_gate: bfloat16 [16, 2048, 768], P('expert', 'dp'), may hold values from -0.125 to 0.125
- w_up: bfloat16 [16, 2048, 768], P('expert', 'dp'), may hold values from -0.125 to 0.125
- w_down: bfloat16 [16, 768, 2048], P('expert', None, 'dp'), may hold values from -0.21875 to 0.21875
Outputs:
- moe_out: bfloat16 [2048, 2048], P(('expert', 'dp'))
Inputs may be any that keep to these rules, and one draw needn't show every extreme that they name: `expert_ids`: each row names 8 different experts. Within the 64 rows of one device no expert is named by more than 48 rows, a bound that some block reaches. swap_flags[0] is 1; the other entries are 0 or 1.
All inputs are finite; a program needn't handle non-finite values.
Results may differ from a plain program's by a relative error of at most 0.0057.
Values may be sent and summed in bfloat16 or wider, within the bound.
A program may use at most 64 MiB of HBM per device.

v0:
```python
import jax
import jax.numpy as jnp
from jax import lax
from jax.sharding import PartitionSpec as P


def on_device(tokens, expert_ids, gate_probs, swap_flags, w_gate, w_up, w_down):
    axis_size = lax.axis_size("expert")
    own_index = lax.axis_index("expert")
    half_span = axis_size // 2
    shares = gate_probs / jnp.sum(gate_probs, axis=1, keepdims=True)
    experts = jnp.arange(axis_size, dtype=jnp.int32)
    dense = jnp.sum(
        jnp.where(expert_ids[:, :, None] == experts[None, None, :], shares[:, :, None], 0.0), axis=1
    )
    lower = own_index < half_span
    own_base = jnp.where(lower, own_index, own_index - half_span)
    own_flag = (
        jnp.sum(jnp.where(jnp.arange(half_span, dtype=jnp.int32) == own_base, swap_flags, 0)) == 1
    )
    served = jnp.where(
        own_flag, jnp.where(lower, own_index + half_span, own_index - half_span), own_index
    )
    rows = lax.all_gather(tokens, "expert", axis=0, tiled=True)
    dense_all = lax.all_gather(dense, "expert", axis=0, tiled=True)
    factor = jnp.sum(jnp.where(experts[None, :] == served, dense_all, 0.0), axis=1)
    gate_next = jnp.dot(
        rows,
        lax.all_gather(w_gate, "dp", axis=1, tiled=True)[0],
        preferred_element_type=jnp.float32,
    )
    up_next = jnp.dot(
        rows, lax.all_gather(w_up, "dp", axis=1, tiled=True)[0], preferred_element_type=jnp.float32
    )
    hidden = (jax.nn.silu(gate_next) * up_next).astype(jnp.bfloat16)
    produced = jnp.dot(
        hidden,
        lax.all_gather(w_down, "dp", axis=2, tiled=True)[0],
        preferred_element_type=jnp.float32,
    ).astype(jnp.bfloat16)
    partial = (factor[:, None] * produced.astype(jnp.float32)).astype(jnp.bfloat16)
    return lax.psum_scatter(partial, "expert", scatter_dimension=0, tiled=True)


def solution(mesh):
    placed = (
        P(("expert", "dp"), None),
        P(("expert", "dp"), None),
        P(("expert", "dp"), None),
        P(),
        P("expert", "dp", None),
        P("expert", "dp", None),
        P("expert", None, "dp"),
    )
    return jax.shard_map(
        on_device, mesh=mesh, in_specs=placed, out_specs=P(("expert", "dp"), None), check_vma=False
    )
```

profile of v0, /device:TPU:0, one launch (start us, length us, event | category | flops | bytes accessed | tf_op | source)
XLA Modules:
  0.0 246.6 jit_solution(10669585378727031929)
XLA Ops:
  6.5 0.0 all-gather.10.cloned.1.call-start
  6.5 0.7 all-gather.10.cloned.1.call-update
  7.3 0.0 all-gather.6.cloned.1.call-start
  7.3 0.7 all-gather.6.cloned.1.call-update
  8.0 0.0 all-gather.8.cloned.1.call-start
  8.1 0.7 all-gather.8.cloned.1.call-update
  8.7 0.0 all-gather.12.cloned.1.call-start
  8.8 0.5 all-gather.12.cloned.1.call-update
  9.3 0.0 reduce-scatter.2.cloned.1.call-start
  9.4 0.0 copy-done
  9.4 0.0 copy-done.1
  9.5 43.1 %all-gather = f32[16,64,16]{1,2,0:T(8,128)S(1)} all-gather(f32[1,64,16]{1,2,0:T(8,128)S(1)} %bitcast.18), channel_id=1, replica_groups=mesh['expert'=16,'dp'=2] {'expert'}, dimensions={0}, use_global_device_ids=true | all-gather | bytes 69632 | tf_op jit(solution)/shard_map/all_gather | solution.py:25
  52.6 0.1 reshape.10
  52.7 0.0 copy-done.2
  52.7 0.6 fusion.9
  54.0 0.1 select_reduce_fusion
  54.1 0.0 all-gather.10.cloned.1.call-done
  54.1 49.5 %all-gather.6.cloned.1.call-done = bf16[1024,2048]{1,0:T(8,128)(2,1)} async-done(((bf16[64,2048]{1,0:T(8,128)(2,1)}), bf16[1024,2048]{1,0:T(8,128)(2,1)}) %all-gather.6.cloned.1.call-update) | async-done | bytes 4194320 | tf_op jit(solution)/shard_map/all_gather | solution.py:24
  103.7 6.1 %fusion.1 = f32[1024,768]{1,0:T(8,128)S(1)} fusion(bf16[1024,2048]{1,0:T(8,128)(2,1)} %all-gather.6.cloned.1.call-done, bf16[1,2048,768]{2,1,0:T(8,128)(2,1)} %all-gather.10.cloned.1.call-done), kind=kOutput, calls=%fused_computation.2 | convolution fusion | flops 3221225472 | bytes 10485760 | tf_op jit(solution)/shard_map/dot_general | solution.py:32
  109.8 6.2 %all-gather.8.cloned.1.call-done = bf16[1,2048,768]{2,1,0:T(8,128)(2,1)} async-done(((bf16[1,1024,768]{2,1,0:T(8,128)(2,1)}), bf16[1,2048,768]{2,1,0:T(8,128)(2,1)}) %all-gather.8.cloned.1.call-update) | async-done | bytes 3145744 | tf_op jit(solution)/shard_map/all_gather | solution.py:29
  116.0 14.7 %all-gather.12.cloned.1.call-done = bf16[1,768,2048]{2,1,0:T(8,128)(2,1)} async-done(((bf16[1,768,1024]{2,1,0:T(8,128)(2,1)}), bf16[1,768,2048]{2,1,0:T(8,128)(2,1)}) %all-gather.12.cloned.1.call-update) | async-done | bytes 3145744 | tf_op jit(solution)/shard_map/all_gather | solution.py:38
  130.7 12.8 %multiply_convert_fusion = bf16[1024,2048]{1,0:T(8,128)(2,1)} fusion(f32[1024]{0:T(1024)S(1)} %select_reduce_fusion, bf16[1,768,2048]{2,1,0:T(8,128)(2,1)} %all-gather.12.cloned.1.call-done, f32[1024,768]{1,0:T(8,128)S(1)} %fusion.1, bf16[1024,2048]{1,0:T(8,128)(2,1)} %all-gather.6.cloned.1.call-done, bf16[1,2048,768]{2,1,0:T(8,128)(2,1)} %all-gather.8.cloned.1.call-done), kind=kOutput, calls=%fused_computation | convolution fusion | flops 6455558144 | bytes 17829888 | tf_op jit(solution)/shard_map/dot_general | solution.py:36
  143.5 0.0 reduce-scatter.2.cloned.1.call-update
  143.6 96.5 %reduce-scatter.2.cloned.1.call-done = bf16[64,2048]{1,0:T(8,128)(2,1)} async-done(((bf16[1024,2048]{1,0:T(8,128)(2,1)}), bf16[64,2048]{1,0:T(8,128)(2,1)}) %reduce-scatter.2.cloned.1.call-update) | async-done | bytes 262160 | tf_op jit(solution)/shard_map/reduce_scatter | solution.py:42
  (8 shorter events, 0.1 us)
Async XLA Ops:
  6.5 2.8 %copy-start = (f32[64,8]{0,1:T(8,128)S(1)}, f32[64,8]{0,1:T(8,128)}, u32[]{:S(2)}) copy-start(f32[64,8]{0,1:T(8,128)} %param.9) | copy-start | bytes 6148
  6.5 2.9 %copy-start.1 = (s32[64,8]{0,1:T(8,128)S(1)}, s32[64,8]{0,1:T(8,128)}, u32[]{:S(2)}) copy-start(s32[64,8]{0,1:T(8,128)} %param.8) | copy-start | bytes 6148
  6.5 46.2 %copy-start.2 = (s32[8]{0:T(128)S(1)}, s32[8]{0:T(128)}, u32[]{:S(2)}) copy-start(s32[8]{0:T(128)} %param.10) | copy-start | bytes 100
  6.5 47.6 %all-gather.10.cloned.1.call-start = ((), (), s32[]{:S(2)}) async-start(), calls=%async_computation.3 | async-start | bytes 4718592 | tf_op jit(solution)/shard_map/all_gather | solution.py:33
  7.3 96.4 %all-gather.6.cloned.1.call-start = ((), (), s32[]{:S(2)}) async-start(), calls=%async_computation.1 | async-start | bytes 4456448 | tf_op jit(solution)/shard_map/all_gather | solution.py:24
  8.0 108.0 %all-gather.8.cloned.1.call-start = ((), (), s32[]{:S(2)}) async-start(), calls=%async_computation.2 | async-start | bytes 4718592 | tf_op jit(solution)/shard_map/all_gather | solution.py:29
  8.7 121.9 %all-gather.12.cloned.1.call-start = ((), (), s32[]{:S(2)}) async-start(), calls=%async_computation.4 | async-start | bytes 4718592 | tf_op jit(solution)/shard_map/all_gather | solution.py:38
  9.3 230.7 %reduce-scatter.2.cloned.1.call-start = ((), (), s32[]{:S(2)}) async-start(), calls=%async_computation.5 | async-start | bytes 4456448 | tf_op jit(solution)/shard_map/reduce_scatter | solution.py:42
Sparse Core Ops, SparseCore 0:
  8.9 14.8 all-gather.9
  26.5 77.0 all-gather.5
  105.2 10.7 all-gather.7
  117.4 13.2 all-gather.11
  143.7 96.3 reduce-scatter.1
where the time goes:
time: 247 us
  waiting for transfers between devices  170 us (69%)
  blocking collectives  43.1 us (17%)
  matrix products  19 us (8%)
  between operations  13.9 us (6%)
    reduce_scatter x1, waiting for transfers between devices, on_device(): return lax.psum_scatter(partial, 'expert', scatter_dimension=0, tiled=True)  96.5 us
    all_gather x1, waiting for transfers between devices, on_device(): rows = lax.all_gather(tokens, 'expert', axis=0, tiled=True)  49.5 us
    all_gather x1, blocking collectives, on_device(): dense_all = lax.all_gather(dense, 'expert', axis=0, tiled=True)  43.1 us
    all_gather x1, waiting for transfers between devices, on_device(): lax.all_gather(w_down, 'dp', axis=2, tiled=True)[0]  14.7 us
    dot_general x1, matrix products, on_device(): jnp.dot(hidden, lax.all_gather(w_down, 'dp', axis=2, tiled=True)[0], pref...  12.8 us
    all_gather x1, waiting for transfers between devices, on_device(): lax.all_gather(w_gate, 'dp', axis=1, tiled=True)[0]  6.18 us
    dot_general x1, matrix products, on_device(): jnp.dot(rows, lax.all_gather(w_up, 'dp', axis=1, tiled=True)[0], preferre...  6.12 us
  transfers between devices with their start and end apart: 5, of which 4 were waited for; matrix products, arithmetic and copies ran while one was open for 3% of the time, Pallas kernels for 0%

commit v1 on v0

--- a/solution.py
+++ b/solution.py
@@ -4,7 +4,31 @@
 from jax.sharding import PartitionSpec as P
 
 
+def supply_all_tasks(mine_x, d_out):
+    mine_x = jnp.moveaxis(mine_x, 0, d_out)
+    b_now = mine_x.shape
+    return mine_x.reshape(*b_now[:d_out], b_now[d_out] * b_now[d_out + 1], *b_now[d_out + 2 :])
+
+
+def guide_domain(patch, row_axis):
+    arr_next = lax.axis_size(row_axis)
+    row_out = lax.axis_index(row_axis)
+    formed, h_now = (arr_next, row_out)
+    res, all_rows = (patch[None], 1)
+    while all_rows < formed:
+        moved = lax.ppermute(res, row_axis, [(it, it ^ all_rows) for it in range(formed)])
+        local_now = h_now & all_rows == 0
+        res = jnp.concatenate([jnp.where(local_now, res, moved), jnp.where(local_now, moved, res)])
+        all_rows *= 2
+    return res
+
+
 def on_device(tokens, expert_ids, gate_probs, swap_flags, w_gate, w_up, w_down):
+
+    def regions_turn(axis_no, in_array, a0):
+        passed = guide_domain(a0, in_array)
+        return supply_all_tasks(passed, axis_no)
+
     axis_size = lax.axis_size("expert")
     own_index = lax.axis_index("expert")
     half_span = axis_size // 2
@@ -22,7 +46,7 @@
         own_flag, jnp.where(lower, own_index + half_span, own_index - half_span), own_index
     )
     rows = lax.all_gather(tokens, "expert", axis=0, tiled=True)
-    dense_all = lax.all_gather(dense, "expert", axis=0, tiled=True)
+    dense_all = regions_turn(0, "expert", dense)
     factor = jnp.sum(jnp.where(experts[None, :] == served, dense_all, 0.0), axis=1)
     gate_next = jnp.dot(
         rows,

time: 247 us -> 247 us (level)
  blocking collectives: 43.1 us -> 0 us
  waiting for transfers between devices: 170 us -> 202 us
  starting transfers between devices: 0.15 us -> 10.5 us
    all_gather x1 -> x0, blocking collectives: 43.1 us -> none  [on_device(): dense_all = lax.all_gather(dense, 'expert', axis=0, tiled=True)]
    all_gather x1, waiting for transfers between devices: 49.5 us -> 76.3 us  [on_device(): rows = lax.all_gather(tokens, 'expert', axis=0, tiled=True)]
    ppermute x0 -> x4, starting transfers between devices: none -> 10.4 us  [guide_domain(): lax.ppermute(res, row_axis, [(it, it ^ all_rows) for it in range(formed)])]
    ppermute x0 -> x4, waiting for transfers between devices: none -> 6.16 us  [guide_domain(): lax.ppermute(res, row_axis, [(it, it ^ all_rows) for it in range(formed)])]
  transfers between devices with their start and end apart: 5 -> 9, of which waited for: 4 -> 8; matrix products, arithmetic and copies ran while one was open for 3% -> 3% of each run, Pallas kernels for 0% -> 0%
where the time goes in v1:
time: 247 us
  waiting for transfers between devices  202 us (82%)
  matrix products  19 us (8%)
  between operations  13.9 us (6%)
  starting transfers between devices  10.5 us (4%)
    reduce_scatter x1, waiting for transfers between devices, on_device(): return lax.psum_scatter(partial, 'expert', scatter_dimension=0, tiled=True)  96.5 us
    all_gather x1, waiting for transfers between devices, on_device(): rows = lax.all_gather(tokens, 'expert', axis=0, tiled=True)  76.3 us
    all_gather x1, waiting for transfers between devices, on_device(): lax.all_gather(w_down, 'dp', axis=2, tiled=True)[0]  14.7 us
    dot_general x1, matrix products, on_device(): jnp.dot(hidden, lax.all_gather(w_down, 'dp', axis=2, tiled=True)[0], pref...  12.8 us
    ppermute x4, starting transfers between devices, guide_domain(): lax.ppermute(res, row_axis, [(it, it ^ all_rows) for it in range(formed)])  10.4 us
    all_gather x1, waiting for transfers between devices, on_device(): lax.all_gather(w_gate, 'dp', axis=1, tiled=True)[0]  6.18 us
    ppermute x4, waiting for transfers between devices, guide_domain(): lax.ppermute(res, row_axis, [(it, it ^ all_rows) for it in range(formed)])  6.16 us
    dot_general x1, matrix products, on_device(): jnp.dot(rows, lax.all_gather(w_up, 'dp', axis=1, tiled=True)[0], preferre...  6.12 us
  transfers between devices with their start and end apart: 9, of which 8 were waited for; matrix products, arithmetic and copies ran while one was open for 3% of the time, Pallas kernels for 0%

profile of v1, /device:TPU:0, one launch (start us, length us, event | category | flops | bytes accessed | tf_op | source)
XLA Modules:
  0.0 246.7 jit_solution(11176733526094126552)
XLA Ops:
  6.5 0.7 all-gather.9.cloned.1.call-update
  7.3 0.0 all-gather.5.cloned.1.call-start
  7.3 0.7 all-gather.5.cloned.1.call-update
  8.0 0.0 all-gather.7.cloned.1.call-start
  8.1 0.7 all-gather.7.cloned.1.call-update
  8.8 0.5 all-gather.11.cloned.1.call-update
  9.3 0.0 reduce-scatter.2.cloned.1.call-start
  9.4 3.0 %collective-permute-start = (f32[1,64,16]{1,2,0:T(8,128)S(1)}, f32[1,64,16]{1,2,0:T(8,128)S(1)}, u32[]{:S(2)}, u32[]{:S(2)}) collective-permute-start(f32[1,64,16]{1,2,0:T(8,128)S(1)} %bitcast.18), channel_id=1, source_target_pairs={{0,2},{2,0},{4,6},{6,4},{8,10},{10,8},{12,14},{14,12},{16,18},{18,... | collective-permute-start | bytes 12296 | tf_op jit(solution)/shard_map/ppermute | solution.py:19
  12.5 1.6 collective-permute-done
  14.1 2.1 collective-permute-start.1
  16.2 1.7 collective-permute-done.1
  17.9 2.1 collective-permute-start.2
  20.1 0.6 fusion.10
  21.4 0.6 collective-permute-done.2
  22.0 3.1 %collective-permute-start.3 = (f32[8,64,16]{1,2,0:T(8,128)S(1)}, f32[8,64,16]{1,2,0:T(8,128)S(1)}, u32[]{:S(2)}, u32[]{:S(2)}) collective-permute-start(f32[8,64,16]{1,2,0:T(8,128)S(1)} %pad_maximum_fusion), channel_id=1, source_target_pairs={{0,16},{2,18},{4,20},{6,22},{8,24},{10,26},{12,28},{14,30},{16,0},... | collective-permute-start | bytes 98312 | tf_op jit(solution)/shard_map/ppermute | solution.py:19
  25.1 2.2 collective-permute-done.3
  27.4 0.1 fusion.9
  27.5 0.1 mul.17
  27.6 76.3 %all-gather.5.cloned.1.call-done = bf16[1024,2048]{1,0:T(8,128)(2,1)} async-done(((bf16[64,2048]{1,0:T(8,128)(2,1)}), bf16[1024,2048]{1,0:T(8,128)(2,1)}) %all-gather.5.cloned.1.call-update) | async-done | bytes 4194320 | tf_op jit(solution)/shard_map/all_gather | solution.py:48
  103.8 6.1 %fusion.1 = f32[1024,768]{1,0:T(8,128)S(1)} fusion(bf16[1024,2048]{1,0:T(8,128)(2,1)} %all-gather.5.cloned.1.call-done, bf16[1,2048,768]{2,1,0:T(8,128)(2,1)} %all-gather.9.cloned.1.call-done), kind=kOutput, calls=%fused_computation.2 | convolution fusion | flops 3221225472 | bytes 10485760 | tf_op jit(solution)/shard_map/dot_general | solution.py:56
  110.0 6.2 %all-gather.7.cloned.1.call-done = bf16[1,2048,768]{2,1,0:T(8,128)(2,1)} async-done(((bf16[1,1024,768]{2,1,0:T(8,128)(2,1)}), bf16[1,2048,768]{2,1,0:T(8,128)(2,1)}) %all-gather.7.cloned.1.call-update) | async-done | bytes 3145744 | tf_op jit(solution)/shard_map/all_gather | solution.py:53
  116.1 14.7 %all-gather.11.cloned.1.call-done = bf16[1,768,2048]{2,1,0:T(8,128)(2,1)} async-done(((bf16[1,768,1024]{2,1,0:T(8,128)(2,1)}), bf16[1,768,2048]{2,1,0:T(8,128)(2,1)}) %all-gather.11.cloned.1.call-update) | async-done | bytes 3145744 | tf_op jit(solution)/shard_map/all_gather | solution.py:62
  130.9 12.8 %multiply_convert_fusion = bf16[1024,2048]{1,0:T(8,128)(2,1)} fusion(f32[1024]{0:T(1024)S(1)} %mul.17, bf16[1,768,2048]{2,1,0:T(8,128)(2,1)} %all-gather.11.cloned.1.call-done, f32[1024,768]{1,0:T(8,128)S(1)} %fusion.1, bf16[1024,2048]{1,0:T(8,128)(2,1)} %all-gather.5.cloned.1.call-done, bf16[1,2048,768]{2,1,0:T(8,128)(2,1)} %all-gather.7.cloned.1.call-done), kind=kOutput, calls=%fused_computation | convolution fusion | flops 6455558144 | bytes 17829888 | tf_op jit(solution)/shard_map/dot_general | solution.py:60
  143.7 96.5 %reduce-scatter.2.cloned.1.call-done = bf16[64,2048]{1,0:T(8,128)(2,1)} async-done(((bf16[1024,2048]{1,0:T(8,128)(2,1)}), bf16[64,2048]{1,0:T(8,128)(2,1)}) %reduce-scatter.2.cloned.1.call-update) | async-done | bytes 262160 | tf_op jit(solution)/shard_map/reduce_scatter | solution.py:66
  (21 shorter events, 0.2 us)
Async XLA Ops:
  6.5 2.8 %copy-start = (f32[64,8]{0,1:T(8,128)S(1)}, f32[64,8]{0,1:T(8,128)}, u32[]{:S(2)}) copy-start(f32[64,8]{0,1:T(8,128)} %param.9) | copy-start | bytes 6148
  6.5 2.9 %copy-start.1 = (s32[64,8]{0,1:T(8,128)S(1)}, s32[64,8]{0,1:T(8,128)}, u32[]{:S(2)}) copy-start(s32[64,8]{0,1:T(8,128)} %param.8) | copy-start | bytes 6148
  6.5 13.5 %copy-start.2 = (s32[8]{0:T(128)S(1)}, s32[8]{0:T(128)}, u32[]{:S(2)}) copy-start(s32[8]{0:T(128)} %param.10) | copy-start | bytes 100
  6.5 21.0 %all-gather.9.cloned.1.call-start = ((), (), s32[]{:S(2)}) async-start(), calls=%async_computation.3 | async-start | bytes 4718592 | tf_op jit(solution)/shard_map/all_gather | solution.py:57
  7.3 96.6 %all-gather.5.cloned.1.call-start = ((), (), s32[]{:S(2)}) async-start(), calls=%async_computation.1 | async-start | bytes 4456448 | tf_op jit(solution)/shard_map/all_gather | solution.py:48
  8.0 108.1 %all-gather.7.cloned.1.call-start = ((), (), s32[]{:S(2)}) async-start(), calls=%async_computation.2 | async-start | bytes 4718592 | tf_op jit(solution)/shard_map/all_gather | solution.py:53
  8.7 122.1 %all-gather.11.cloned.1.call-start = ((), (), s32[]{:S(2)}) async-start(), calls=%async_computation.4 | async-start | bytes 4718592 | tf_op jit(solution)/shard_map/all_gather | solution.py:62
  9.3 230.9 %reduce-scatter.2.cloned.1.call-start = ((), (), s32[]{:S(2)}) async-start(), calls=%async_computation.5 | async-start | bytes 4456448 | tf_op jit(solution)/shard_map/reduce_scatter | solution.py:66
  9.4 4.6 %collective-permute-start = (f32[1,64,16]{1,2,0:T(8,128)S(1)}, f32[1,64,16]{1,2,0:T(8,128)S(1)}, u32[]{:S(2)}, u32[]{:S(2)}) collective-permute-start(f32[1,64,16]{1,2,0:T(8,128)S(1)} %bitcast.18), channel_id=1, source_target_pairs={{0,2},{2,0},{4,6},{6,4},{8,10},{10,8},{12,14},{14,12},{16,18},{18,... | collective-permute-start | bytes 12296 | tf_op jit(solution)/shard_map/ppermute | solution.py:19
  14.1 3.8 %collective-permute-start.1 = (f32[2,64,16]{1,2,0:T(8,128)S(1)}, f32[2,64,16]{1,2,0:T(8,128)S(1)}, u32[]{:S(2)}, u32[]{:S(2)}) collective-permute-start(f32[2,64,16]{1,2,0:T(8,128)S(1)} %pad_maximum_fusion.2), channel_id=1, source_target_pairs={{0,4},{2,6},{4,0},{6,2},{8,12},{10,14},{12,8},{14,10},{16,20},{18,... | collective-permute-start | bytes 24584 | tf_op jit(solution)/shard_map/ppermute | solution.py:19
  17.9 4.0 %collective-permute-start.2 = (f32[4,64,16]{1,2,0:T(8,128)S(1)}, f32[4,64,16]{1,2,0:T(8,128)S(1)}, u32[]{:S(2)}, u32[]{:S(2)}) collective-permute-start(f32[4,64,16]{1,2,0:T(8,128)S(1)} %pad_maximum_fusion.1), channel_id=1, source_target_pairs={{0,8},{2,10},{4,12},{6,14},{8,0},{10,2},{12,4},{14,6},{16,24},{18,... | collective-permute-start | bytes 49160 | tf_op jit(solution)/shard_map/ppermute | solution.py:19
  22.0 5.4 %collective-permute-start.3 = (f32[8,64,16]{1,2,0:T(8,128)S(1)}, f32[8,64,16]{1,2,0:T(8,128)S(1)}, u32[]{:S(2)}, u32[]{:S(2)}) collective-permute-start(f32[8,64,16]{1,2,0:T(8,128)S(1)} %pad_maximum_fusion), channel_id=1, source_target_pairs={{0,16},{2,18},{4,20},{6,22},{8,24},{10,26},{12,28},{14,30},{16,0},... | collective-permute-start | bytes 98312 | tf_op jit(solution)/shard_map/ppermute | solution.py:19
Sparse Core Ops, SparseCore 0:
  8.9 14.8 all-gather.8
  26.5 77.2 all-gather.4
  105.4 10.7 all-gather.6
  117.5 13.2 all-gather.10
  143.8 96.3 reduce-scatter.1
